TPU v7x, 256 devices: a whole 4x4x8 slice. The times are simulated.
256 devices in a mesh: seq: 64 (over y, z, x_hi), ch: 4 (over x_lo, core).
Axes of the slice: x: 4 (x_hi: 2, x_lo: 2; x = x_hi * 2 + x_lo), y: 4, z: 8, core: 2. Of those that a mesh axis runs over, the one named last changes fastest.
Arguments:
- value_in: bfloat16 [4096, 8192], P('ch', 'seq'), may hold values from -6 to 6
- gate_inner: bfloat16 [4096, 8192], P('ch', 'seq'), may hold values from -6 to 6
- gate_outer: bfloat16 [4096, 8192], P('ch', 'seq'), may hold values from -6 to 6
- out_grad: bfloat16 [4096, 8192], P('ch', 'seq'), may hold values from -6 to 6
- filter_proj: bfloat16 [2, 4096, 64], P(None, 'ch'), may hold values from -0.75 to 0.75
- decay: float32 [2, 4096], P(None, 'ch'), may hold values from 6.1035156e-05 to 0.05
- frequency: float32 [64], replicated, may hold values from 0.001 to 3
Outputs:
- grad_value: bfloat16 [4096, 8192], P('ch', 'seq')
- grad_gate_inner: bfloat16 [4096, 8192], P('ch', 'seq')
- grad_gate_outer: bfloat16 [4096, 8192], P('ch', 'seq')
- filter_grad: float32 [2, 4096, 64], P(None, 'ch')
All inputs are finite; a program needn't handle non-finite values.
Results may differ from a plain program's by a relative error of at most 0.0025.
Values may be sent and summed in bfloat16 or wider, within the bound.
A program may use at most 64 MiB of HBM per device.

v0:
```python
import functools
from types import SimpleNamespace

import jax
import jax.numpy as jnp
from jax import lax
from jax.experimental import pallas as pl
from jax.experimental.pallas import tpu as pltpu
from jax.sharding import PartitionSpec as P

MESH = pl.DeviceIdType.MESH
f32, bf16 = jnp.float32, jnp.bfloat16
T = 128
N = 64
CH = 16
G = 8
GROUPS = CH // G
HALF = N // 2
ROWS = N * G
F = 64
NN = (((1,), (0,)), ((), ()))
NT = (((1,), (1,)), ((), ()))


def dg(a, b, dims=NN):
    return lax.dot_general(a, b, dims, preferred_element_type=f32)


def split(x):
    hi = x.astype(bf16)
    return hi, (x - hi.astype(f32)).astype(bf16)


def dot3(a, bh, bl, dims=NN):
    ah, al = split(a)
    return dg(ah, bh, dims) + (dg(al, bh, dims) + dg(ah, bl, dims))


def lanes(shape):
    return lax.broadcasted_iota(jnp.int32, shape, len(shape) - 1)


def rows_iota(shape):
    return lax.broadcasted_iota(jnp.int32, shape, 0)


def prepare(first, proj_ref, decay_ref, freq_ref, s):
    pick = lanes((CH, decay_ref.shape[1])) == rows_iota((CH, decay_ref.shape[1])) + first
    one_hot = pick.astype(f32).astype(bf16)
    low = lanes((T, T)) < F
    freq = jnp.concatenate([freq_ref[...], freq_ref[...]], 1)
    pos = rows_iota((T, T)).astype(f32)
    for which, num in ((0, (T - 1.0) - pos), (1, pos + 2.0)):
        angle = freq * num
        cos, sin = jnp.cos(angle), jnp.sin(angle)
        zero = jnp.zeros_like(cos)
        for half, keep in ((0, low), (1, jnp.logical_not(low))):
            for part, val in ((0, cos), (1, sin)):
                hi, lo = split(jnp.where(keep, val, zero))
                at = (which, pl.ds(half * T, T), pl.ds(part * T, T))
                s.basis_hi[at] = hi
                s.basis_lo[at] = lo
    fh, fl = split(jnp.sin(freq * (pos + 1.0)))
    s.feat_hi[...] = fh
    s.feat_lo[...] = fl
    s.flip[...] = (lanes((T, T)) + rows_iota((T, T)) == T - 1).astype(f32).astype(bf16)
    lane = lanes((CH, T)).astype(f32)
    turn = freq * float(T)
    turn_cos, turn_sin = jnp.cos(turn), jnp.sin(turn)
    for k in (0, 1):
        rate = jnp.sum(jnp.where(pick, decay_ref[pl.ds(k, 1), :], 0.0), axis=1, keepdims=True)
        rate = jnp.broadcast_to(rate, (CH, T))
        gain = jnp.sqrt(2.0 * rate)
        weights = dg(one_hot, proj_ref[k], NT)
        weights = jnp.concatenate([weights, weights], 1)
        window = gain * jnp.exp(-rate * lane)
        head = jnp.where(lanes((CH, T)) < F, weights, 0.0).astype(bf16)
        taps = (dg(head, fh, NT) + dg(head, fl, NT)) * window
        shrink = jnp.exp(-rate * float(T))
        for name, val in (
            ("gain", gain),
            ("weight", weights * gain),
            ("window", window),
            ("taps", taps),
            ("near", jnp.exp(-rate * ((T - 1.0) - lane))),
            ("far", jnp.exp(-rate * (lane + 1.0))),
            ("turn_re", shrink * turn_cos),
            ("turn_im", shrink * turn_sin),
        ):
            getattr(s, name)[k] = val
    ahead = lanes((T, T)) >= rows_iota((T, T))

    def toeplitz(i, _):
        k, d = i // CH, lax.rem(i, CH)
        row = jnp.broadcast_to(s.taps[k, pl.ds(d, 1), :], (T, T))
        mat = jnp.where(ahead, pltpu.roll(row, 0, 1, stride=1, stride_axis=0), 0.0)
        hi, lo = split(mat)
        s.toep_hi[i] = hi
        s.toep_lo[i] = lo
        return 0

    lax.fori_loop(0, 2 * CH, toeplitz, 0, unroll=2)


def of_channel(d):
    return pl.ds(d, N, stride=G)


def group_rows(g):
    return pl.ds(pl.multiple_of(g * G, G), G)


def over_chunks(x, row):
    n, m = x.shape[0] // G, x.shape[1]
    return (x.reshape(n, G, m) * row[None]).reshape(n * G, m)


def modal(x, weight, which, out, s):
    scaled = over_chunks(x, weight)
    scaled = jnp.concatenate([scaled[: ROWS // 2], scaled[ROWS // 2 :]], 1)
    out[...] = dot3(scaled, s.basis_hi[which], s.basis_lo[which])


def scan(src, dst, re, im, backward):
    def at(c):
        c = HALF - 1 - c if backward else c
        return pl.ds(pl.multiple_of(c * G, G), G)

    def step(store, c, carry):
        zr, zi = carry
        rows = at(c)
        if store:
            dst[rows, :T] = zr
            dst[rows, T:] = zi
        return (re * zr - im * zi) + src[rows, :T], (re * zi + im * zr) + src[rows, T:]

    zero = jnp.zeros((G, T), f32)
    end = lax.fori_loop(0, HALF, functools.partial(step, False), (zero, zero), unroll=8)
    late = lanes((G, T)) < F if backward else lanes((G, T)) >= F
    begin = tuple(jnp.where(late, pltpu.roll(x, F, 1), 0.0) for x in end)
    lax.fori_loop(0, HALF, functools.partial(step, True), begin, unroll=8)


def carried(state, weight, decay, which, s):
    z = jnp.concatenate([over_chunks(state[:, T:], weight), over_chunks(state[:, :T], weight)], 1)
    y = dot3(z, s.basis_hi[which], s.basis_lo[which], NT)
    return over_chunks(jnp.concatenate([y[:, :T], y[:, T:]], 0), decay)


def conv(k, g, x, exact, s):
    grow = group_rows(g)
    modal(x[...], s.near[k, grow, :], 0, s.local, s)
    scan(s.local, s.state.at[k], s.turn_re[k, grow, :], s.turn_im[k, grow, :], False)

    def channel(d, _):
        i = k * CH + g * G + d
        xh, xl = split(x[of_channel(d), :])
        y = dg(xh, s.toep_hi[i]) + dg(xh, s.toep_lo[i])
        if not exact:
            y = y + dg(xl, s.toep_hi[i])
        s.y[of_channel(d), :] = y
        return 0

    lax.fori_loop(0, G, channel, 0, unroll=4)
    return s.y[...] + carried(s.state[k], s.weight[k, grow, :], s.far[k, grow, :], 1, s)


def corr(k, g, x, signal, exact, s):
    grow = group_rows(g)
    modal(x[...], s.far[k, grow, :], 1, s.local, s)
    scan(s.local, s.back, s.turn_re[k, grow, :], s.turn_im[k, grow, :], True)

    def channel(d, _):
        i = k * CH + g * G + d
        xh, xl = split(x[of_channel(d), :])
        th = s.toep_hi[i]
        s.y[of_channel(d), :] = dg(xh, th, NT) + dg(xl, th, NT) + dg(xh, s.toep_lo[i], NT)
        vh, vl = split(signal[of_channel(d), :])
        if exact:
            left, right = [vh, vh], [xh, xl]
        else:
            left, right = [vh, vl, vh], [xh, xh, xl]
        turned = dg(s.flip[...], jnp.concatenate(left, 0), NT).astype(bf16)
        pairs = dg(turned, jnp.concatenate(right, 0))
        pairs = pltpu.roll(pairs, 1, 1, stride=1, stride_axis=0)
        pairs = jnp.where(lanes((T, T)) <= rows_iota((T, T)), pairs, 0.0)
        s.lag[pl.ds(d, 1), :] = jnp.sum(pairs, axis=0, keepdims=True)
        return 0

    lax.fori_loop(0, G, channel, 0, unroll=4)
    both = s.local[:, :T] * s.state[k, :, T:] + s.local[:, T:] * s.state[k, :, :T]
    both = jnp.sum(both.reshape(HALF, G, T), axis=0)
    both = both + pltpu.roll(both, F, 1)
    grad = dot3(s.lag[...] * s.window[k, grow, :], s.feat_hi[...], s.feat_lo[...])
    grad = grad + both * s.gain[k, grow, :]
    y = s.y[...] + carried(s.back, s.weight[k, grow, :], s.near[k, grow, :], 0, s)
    return y, grad


def compute_group(g, load, send, s):
    s.v[...] = load(0)
    inner_act = conv(0, g, s.v, True, s)
    s.act[...] = inner_act
    s.mixed[...] = load(1) * inner_act
    outer_act = conv(1, g, s.mixed, False, s)
    out_grad = load(3)
    send(2, out_grad * outer_act)
    s.x[...] = out_grad * load(2)
    grad_mixed, grad_outer = corr(1, g, s.x, s.mixed, False, s)
    send(1, grad_mixed * s.act[...])
    s.x[...] = grad_mixed * load(1)
    grad_value, grad_inner = corr(0, g, s.x, s.v, True, s)
    send(0, grad_value)
    s.own[group_rows(g), :] = jnp.where(lanes((G, T)) < F, grad_inner, grad_outer)


COMPUTE_SCRATCH = dict(
    basis_hi=((2, 2 * T, 2 * T), bf16),
    basis_lo=((2, 2 * T, 2 * T), bf16),
    feat_hi=((T, T), bf16),
    feat_lo=((T, T), bf16),
    flip=((T, T), bf16),
    gain=((2, CH, T), f32),
    weight=((2, CH, T), f32),
    window=((2, CH, T), f32),
    taps=((2, CH, T), f32),
    near=((2, CH, T), f32),
    far=((2, CH, T), f32),
    turn_re=((2, CH, T), f32),
    turn_im=((2, CH, T), f32),
    toep_hi=((2 * CH, T, T), bf16),
    toep_lo=((2 * CH, T, T), bf16),
    local=((ROWS // 2, 2 * T), f32),
    state=((2, ROWS // 2, 2 * T), f32),
    back=((ROWS // 2, 2 * T), f32),
    v=((ROWS, T), f32),
    mixed=((ROWS, T), f32),
    act=((ROWS, T), f32),
    x=((ROWS, T), f32),
    y=((ROWS, T), f32),
    lag=((G, T), f32),
    own=((CH, T), f32),
)


def remote(src, dst, send, recv, **where):
    return pltpu.make_async_remote_copy(
        src_ref=src, dst_ref=dst, send_sem=send, recv_sem=recv, device_id=where, device_id_type=MESH
    )


def await_bytes(ref, sem):
    pltpu.make_async_copy(ref, ref, sem).wait()


def kernel(names, quarter, *refs):
    inputs, refs = refs[:4], refs[4:]
    proj_ref, decay_ref, freq_ref = refs[:3]
    outputs, grad_ref, refs = refs[3:6], refs[6], refs[7:]
    s = SimpleNamespace(**dict(zip(names, refs)))
    me, mine = lax.axis_index("seq"), lax.axis_index("ch")
    mx, mz, my = lax.rem(me, 2), lax.rem(me // 2, 8), me // 16

    barrier = pltpu.get_barrier_semaphore()

    def greet(j, _):
        pl.semaphore_signal(
            barrier, inc=1, device_id={"seq": lax.rem(me + j, N)}, device_id_type=MESH
        )
        return 0

    lax.fori_loop(1, N, greet, 0)
    for j in range(1, quarter):
        pl.semaphore_signal(
            barrier, inc=1, device_id={"ch": lax.rem(mine + j, quarter)}, device_id_type=MESH
        )
    pl.semaphore_wait(barrier, N - 1 + quarter - 1)

    def block_rows(p, g):
        return pl.ds(pl.multiple_of(p * CH + g * G, G), G)

    for g in range(GROUPS):
        for i in (0, 1, 3, 2):

            def push(j, _, g=g, i=i):
                p = lax.rem(me + j, N)
                remote(
                    inputs[i].at[block_rows(p, g), :],
                    s.came.at[i, g, me],
                    s.in_send.at[i, g],
                    s.in_recv.at[i, g],
                    seq=p,
                ).start()
                return 0

            lax.fori_loop(1, N, push, 0)
            pltpu.make_async_copy(
                inputs[i].at[block_rows(me, g), :], s.came.at[i, g, me], s.in_recv.at[i, g]
            ).start()

    prepare(me * CH, proj_ref, decay_ref, freq_ref, s)

    def group(g, _):
        here = set()

        def load(i):
            if i not in here:
                here.add(i)
                await_bytes(s.came.at[i, g], s.in_recv.at[i, g])
            return s.came[i, g].reshape(ROWS, T).astype(f32)

        def send(i, val):
            s.goes[i, g] = val.astype(bf16).reshape(N, G, T)

            def push(j, _):
                p = lax.rem(me + j, N)
                remote(
                    s.goes.at[i, g, p],
                    outputs[i].at[block_rows(me, g), :],
                    s.out_send.at[i, g],
                    s.out_recv.at[i],
                    seq=p,
                ).start()
                return 0

            lax.fori_loop(1, N, push, 0)
            pltpu.make_async_copy(
                s.goes.at[i, g, me], outputs[i].at[block_rows(me, g), :], s.out_recv.at[i]
            ).start()

        compute_group(g, load, send, s)
        return 0

    lax.fori_loop(0, GROUPS, group, 0)

    s.every[mx, my, mz] = s.own[...]
    for j in range(1, 8):
        z = lax.rem(mz + j, 8)
        spot = s.every.at[mx, my, mz]
        remote(spot, spot, s.share_send.at[0], s.share_recv.at[0], seq=my * 16 + z * 2 + mx).start()
    await_bytes(s.every.at[0, 0, pl.ds(0, 7)], s.share_recv.at[0])
    for j in range(1, 4):
        y = lax.rem(my + j, 4)
        spot = s.every.at[mx, my]
        remote(spot, spot, s.share_send.at[1], s.share_recv.at[1], seq=y * 16 + mz * 2 + mx).start()
    await_bytes(s.every.at[0, pl.ds(0, 3)], s.share_recv.at[1])
    spot = s.every.at[mx]
    remote(spot, spot, s.share_send.at[2], s.share_recv.at[2], seq=my * 16 + mz * 2 + 1 - mx).start()
    await_bytes(s.every.at[0], s.share_recv.at[2])

    grads = s.every[...]
    square = jnp.sum((grads * grads).reshape(N * CH // 8, 8, T), axis=0)
    s.square[mine] = square
    for j in range(1, quarter):
        spot = s.square.at[mine]
        remote(
            spot, spot, s.share_send.at[3], s.share_recv.at[3], ch=lax.rem(mine + j, quarter)
        ).start()
    await_bytes(s.square.at[pl.ds(0, quarter - 1)], s.share_recv.at[3])
    total = jnp.sum(s.square[...], axis=(0, 1), keepdims=True)[0]
    total = jnp.sum(total, axis=1, keepdims=True)
    scale = lax.rsqrt(total / float(2 * F * CH * N * quarter) + 1e-06)
    for y in range(4):
        for z in range(8):
            for x in range(2):
                p = y * 16 + z * 2 + x
                grad_ref[pl.ds(p * CH, CH), :] = s.every[x, y, z] * scale

    for i in range(3):
        await_bytes(outputs[i], s.out_recv.at[i])
    for g in range(GROUPS):
        for i in range(4):
            await_bytes(s.came.at[i, g, pl.ds(0, N - 1)], s.in_send.at[i, g])
        for i in range(3):
            await_bytes(s.goes.at[i, g, pl.ds(0, N - 1)], s.out_send.at[i, g])
    await_bytes(s.every.at[0, 0, pl.ds(0, 7)], s.share_send.at[0])
    await_bytes(s.every.at[0, pl.ds(0, 3)], s.share_send.at[1])
    await_bytes(s.every.at[0], s.share_send.at[2])
    await_bytes(s.square.at[pl.ds(0, quarter - 1)], s.share_send.at[3])


def body(quarter, value_in, gate_inner, gate_outer, out_grad, filter_proj, decay, frequency):
    scratch = {name: pltpu.VMEM(*spec) for name, spec in COMPUTE_SCRATCH.items()}
    scratch |= dict(
        came=pltpu.VMEM((4, GROUPS, N, G, T), bf16),
        goes=pltpu.VMEM((3, GROUPS, N, G, T), bf16),
        every=pltpu.VMEM((2, 4, 8, CH, T), f32),
        square=pltpu.VMEM((quarter, 8, T), f32),
        in_send=pltpu.SemaphoreType.DMA((4, GROUPS)),
        in_recv=pltpu.SemaphoreType.DMA((4, GROUPS)),
        out_send=pltpu.SemaphoreType.DMA((3, GROUPS)),
        out_recv=pltpu.SemaphoreType.DMA((3,)),
        share_send=pltpu.SemaphoreType.DMA((4,)),
        share_recv=pltpu.SemaphoreType.DMA((4,)),
    )
    local = jax.ShapeDtypeStruct(value_in.shape, bf16)
    anywhere, vmem = pl.BlockSpec(memory_space=pl.ANY), pl.BlockSpec(memory_space=pltpu.VMEM)
    grad_value, grad_inner, grad_outer, grads = pl.pallas_call(
        functools.partial(kernel, tuple(scratch), quarter),
        out_shape=(local, local, local, jax.ShapeDtypeStruct((N * CH, T), f32)),
        in_specs=[anywhere] * 4 + [vmem] * 3,
        out_specs=[anywhere] * 3 + [vmem],
        scratch_shapes=list(scratch.values()),
        compiler_params=pltpu.CompilerParams(
            collective_id=0, has_side_effects=True, vmem_limit_bytes=40 << 20
        ),
    )(
        value_in,
        gate_inner,
        gate_outer,
        out_grad,
        jnp.transpose(filter_proj, (0, 2, 1)),
        decay,
        frequency.reshape(1, F),
    )
    filter_grad = jnp.transpose(grads.reshape(N * CH, 2, F), (1, 0, 2))
    return grad_value, grad_inner, grad_outer, filter_grad


def solution(mesh):
    placed = (P("ch", "seq"),) * 4 + (P(None, "ch", None), P(None, "ch"), P())
    return jax.shard_map(
        functools.partial(body, mesh.shape["ch"]),
        mesh=mesh,
        in_specs=placed,
        out_specs=(P("ch", "seq"),) * 3 + (P(None, "ch", None),),
        check_vma=False,
    )
```

profile of v0, /device:TPU:1, one launch (start us, length us, event | category | flops | bytes accessed | tf_op | source)
XLA Modules:
  0.0 79.3 jit_solution(15381253338042831069)
XLA Ops:
  0.6 0.0 copy-start.6
  0.6 0.6 copy-done.6
  1.3 0.0 copy-start
  1.3 0.9 %copy-done = bf16[1024,128]{1,0:T(8,128)(2,1)S(1)} copy-done((bf16[1024,128]{1,0:T(8,128)(2,1)S(1)}, bf16[1024,128]{1,0:T(8,128)(2,1)}, u32[]{:S(2)}) %copy-start) | copy-done | bytes 262168
  2.2 0.0 copy-start.1
  2.2 0.9 %copy-done.1 = bf16[1024,128]{1,0:T(8,128)(2,1)S(1)} copy-done((bf16[1024,128]{1,0:T(8,128)(2,1)S(1)}, bf16[1024,128]{1,0:T(8,128)(2,1)}, u32[]{:S(2)}) %copy-start.1) | copy-done | bytes 262168
  3.2 0.0 copy-start.2
  3.2 0.9 %copy-done.2 = bf16[1024,128]{1,0:T(8,128)(2,1)S(1)} copy-done((bf16[1024,128]{1,0:T(8,128)(2,1)S(1)}, bf16[1024,128]{1,0:T(8,128)(2,1)}, u32[]{:S(2)}) %copy-start.2) | copy-done | bytes 262168
  4.1 0.0 copy-start.3
  4.1 0.9 %copy-done.3 = bf16[1024,128]{1,0:T(8,128)(2,1)S(1)} copy-done((bf16[1024,128]{1,0:T(8,128)(2,1)S(1)}, bf16[1024,128]{1,0:T(8,128)(2,1)}, u32[]{:S(2)}) %copy-start.3) | copy-done | bytes 262168
  5.1 0.0 copy-start.4
  5.1 0.9 %copy-done.4 = bf16[2,1024,64]{1,2,0:T(8,128)(2,1)S(1)} copy-done((bf16[2,1024,64]{1,2,0:T(8,128)(2,1)S(1)}, bf16[2,1024,64]{1,2,0:T(8,128)(2,1)}, u32[]{:S(2)}) %copy-start.4) | copy-done | bytes 262168
  6.0 0.0 copy-start.5
  6.0 0.7 copy-done.5
  6.7 69.5 %shard_map.102 = (bf16[1024,128]{1,0:T(8,128)(2,1)S(1)}, bf16[1024,128]{1,0:T(8,128)(2,1)S(1)}, bf16[1024,128]{1,0:T(8,128)(2,1)S(1)}, f32[1024,128]{1,0:T(8,128)S(1)}) custom-call(bf16[1024,128]{1,0:T(8,128)(2,1)S(1)} %copy-done, bf16[1024,128]{1,0:T(8,128)(2,1)S(1)} %copy-done.1, bf16[1024,128]{1,0:T(8,128)(2,1)S(1)} %copy-done.2, ...), custom_call_target="tpu_custom_call" | custom-call | tf_op jit(solution)/shard_map/pallas_call | solution.py:398
  76.2 1.0 %copy.12 = f32[1024,128]{0,1:T(8,128)} copy(f32[1024,128]{1,0:T(8,128)S(1)} %get-tuple-element.11) | data formatting | bytes 1048576 | tf_op jit(solution)/shard_map/pallas_call | solution.py:398
  77.2 0.7 copy.16
  77.9 0.7 copy.17
  78.6 0.7 copy.18
Async XLA Ops:
  0.6 0.7 copy-start.6
  1.3 0.9 %copy-start = (bf16[1024,128]{1,0:T(8,128)(2,1)S(1)}, bf16[1024,128]{1,0:T(8,128)(2,1)}, u32[]{:S(2)}) copy-start(bf16[1024,128]{1,0:T(8,128)(2,1)} %refs_0_.1) | copy-start | bytes 786436
  2.2 0.9 %copy-start.1 = (bf16[1024,128]{1,0:T(8,128)(2,1)S(1)}, bf16[1024,128]{1,0:T(8,128)(2,1)}, u32[]{:S(2)}) copy-start(bf16[1024,128]{1,0:T(8,128)(2,1)} %refs_1_.1) | copy-start | bytes 786436
  3.2 0.9 %copy-start.2 = (bf16[1024,128]{1,0:T(8,128)(2,1)S(1)}, bf16[1024,128]{1,0:T(8,128)(2,1)}, u32[]{:S(2)}) copy-start(bf16[1024,128]{1,0:T(8,128)(2,1)} %refs_2_.1) | copy-start | bytes 786436
  4.1 0.9 %copy-start.3 = (bf16[1024,128]{1,0:T(8,128)(2,1)S(1)}, bf16[1024,128]{1,0:T(8,128)(2,1)}, u32[]{:S(2)}) copy-start(bf16[1024,128]{1,0:T(8,128)(2,1)} %refs_3_.1) | copy-start | bytes 786436
  5.1 0.9 %copy-start.4 = (bf16[2,1024,64]{1,2,0:T(8,128)(2,1)S(1)}, bf16[2,1024,64]{1,2,0:T(8,128)(2,1)}, u32[]{:S(2)}) copy-start(bf16[2,1024,64]{1,2,0:T(8,128)(2,1)} %param.11) | copy-start | bytes 786436
  6.0 0.7 copy-start.5
where the time goes:
time: 79.6 us; the launch traced here: 79.3 us
  Pallas kernels  69.5 us (87%)
  local copies, waits for them, and re-layouts  9.19 us (12%)
    pallas_call x1, Pallas kernels, body(): pl.pallas_call(functools.partial(kernel, tuple(scratch), quarter), out_sh...  69.5 us
    unnamed x17, local copies, waits for them, and re-layouts  8.2 us

commit v1 on v0

--- a/solution.py
+++ b/solution.py
@@ -211,7 +211,7 @@
     s.x[...] = grad_mixed * load(1)
     grad_value, grad_inner = corr(0, g, s.x, s.v, True, s)
     send(0, grad_value)
-    s.own[group_rows(g), :] = jnp.where(lanes((G, T)) < F, grad_inner, grad_outer)
+    return jnp.where(lanes((G, T)) < F, grad_inner, grad_outer)
 
 
 COMPUTE_SCRATCH = dict(
@@ -239,7 +239,6 @@
     x=((ROWS, T), f32),
     y=((ROWS, T), f32),
     lag=((G, T), f32),
-    own=((CH, T), f32),
 )
 
 
@@ -255,12 +254,15 @@
 
 def kernel(names, quarter, *refs):
     inputs, refs = refs[:4], refs[4:]
-    proj_ref, decay_ref, freq_ref = refs[:3]
+    small = refs[:3]
     outputs, grad_ref, refs = refs[3:6], refs[6], refs[7:]
     s = SimpleNamespace(**dict(zip(names, refs)))
     me, mine = lax.axis_index("seq"), lax.axis_index("ch")
     mx, mz, my = lax.rem(me, 2), lax.rem(me // 2, 8), me // 16
 
+    tables = (s.proj, s.decay, s.freq)
+    for i in range(3):
+        pltpu.make_async_copy(small[i], tables[i], s.table_sem.at[i]).start()
     barrier = pltpu.get_barrier_semaphore()
 
     def greet(j, _):
@@ -269,17 +271,27 @@
         )
         return 0
 
-    lax.fori_loop(1, N, greet, 0)
-    for j in range(1, quarter):
-        pl.semaphore_signal(
-            barrier, inc=1, device_id={"ch": lax.rem(mine + j, quarter)}, device_id_type=MESH
-        )
-    pl.semaphore_wait(barrier, N - 1 + quarter - 1)
+    def layer(j):
+        return dict(seq=lax.rem(j, 4) * 16 + mz * 2 + lax.rem(j // 4, 2), ch=j // 8)
+
+    def greet_layer(j, _):
+        spot = layer(lax.rem(mine * 8 + j, layer_size))
+        pl.semaphore_signal(barrier, inc=1, device_id=spot, device_id_type=MESH)
+        return 0
+
+    layer_size = 8 * quarter
+    lax.fori_loop(1, N, greet, 0, unroll=9)
+    lax.fori_loop(8, layer_size, greet_layer, 0, unroll=8)
+    pl.semaphore_wait(barrier, N - 1 + layer_size - 8)
 
     def block_rows(p, g):
         return pl.ds(pl.multiple_of(p * CH + g * G, G), G)
 
     for g in range(GROUPS):
+        if g == 1:
+            for i in range(3):
+                pltpu.make_async_copy(small[i], tables[i], s.table_sem.at[i]).wait()
+            prepare(me * CH, *tables, s)
         for i in (0, 1, 3, 2):
 
             def push(j, _, g=g, i=i):
@@ -293,78 +305,87 @@
                 ).start()
                 return 0
 
-            lax.fori_loop(1, N, push, 0)
+            lax.fori_loop(1, N, push, 0, unroll=9)
             pltpu.make_async_copy(
                 inputs[i].at[block_rows(me, g), :], s.came.at[i, g, me], s.in_recv.at[i, g]
             ).start()
 
-    prepare(me * CH, proj_ref, decay_ref, freq_ref, s)
-
-    def group(g, _):
+    def push_out(i, g):
+        def push(j, _):
+            p = lax.rem(me + j, N)
+            remote(
+                s.goes.at[i, g, p],
+                outputs[i].at[block_rows(me, g), :],
+                s.out_send.at[i, g],
+                s.out_recv.at[i],
+                seq=p,
+            ).start()
+            return 0
+
+        lax.fori_loop(1, N, push, 0, unroll=9)
+        pltpu.make_async_copy(
+            s.goes.at[i, g, me], outputs[i].at[block_rows(me, g), :], s.out_recv.at[i]
+        ).start()
+
+    def share_column(g):
+        spot = s.every.at[g, mx * 4 + my, mz]
+        for j in range(1, 8):
+            seq = my * 16 + lax.rem(mz + j, 8) * 2 + mx
+            remote(spot, spot, s.share_send.at[0, g], s.share_recv.at[0, g], seq=seq).start()
+
+    def share_layer(g):
+        await_bytes(s.every.at[g, 0, pl.ds(0, 7)], s.share_recv.at[0, g])
+        spot = s.every.at[g, mx * 4 + my]
+        for j in range(1, 8):
+            seq = layer(lax.rem(mx * 4 + my + j, 8))["seq"]
+            remote(spot, spot, s.share_send.at[1, g], s.share_recv.at[1, g], seq=seq).start()
+
+    for g in range(GROUPS):
+        last = g == GROUPS - 1
         here = set()
 
-        def load(i):
+        def load(i, g=g, here=here):
             if i not in here:
                 here.add(i)
                 await_bytes(s.came.at[i, g], s.in_recv.at[i, g])
             return s.came[i, g].reshape(ROWS, T).astype(f32)
 
-        def send(i, val):
+        def send(i, val, g=g, last=last):
             s.goes[i, g] = val.astype(bf16).reshape(N, G, T)
-
-            def push(j, _):
-                p = lax.rem(me + j, N)
-                remote(
-                    s.goes.at[i, g, p],
-                    outputs[i].at[block_rows(me, g), :],
-                    s.out_send.at[i, g],
-                    s.out_recv.at[i],
-                    seq=p,
-                ).start()
-                return 0
-
-            lax.fori_loop(1, N, push, 0)
-            pltpu.make_async_copy(
-                s.goes.at[i, g, me], outputs[i].at[block_rows(me, g), :], s.out_recv.at[i]
-            ).start()
-
-        compute_group(g, load, send, s)
-        return 0
-
-    lax.fori_loop(0, GROUPS, group, 0)
-
-    s.every[mx, my, mz] = s.own[...]
-    for j in range(1, 8):
-        z = lax.rem(mz + j, 8)
-        spot = s.every.at[mx, my, mz]
-        remote(spot, spot, s.share_send.at[0], s.share_recv.at[0], seq=my * 16 + z * 2 + mx).start()
-    await_bytes(s.every.at[0, 0, pl.ds(0, 7)], s.share_recv.at[0])
-    for j in range(1, 4):
-        y = lax.rem(my + j, 4)
-        spot = s.every.at[mx, my]
-        remote(spot, spot, s.share_send.at[1], s.share_recv.at[1], seq=y * 16 + mz * 2 + mx).start()
-    await_bytes(s.every.at[0, pl.ds(0, 3)], s.share_recv.at[1])
-    spot = s.every.at[mx]
-    remote(spot, spot, s.share_send.at[2], s.share_recv.at[2], seq=my * 16 + mz * 2 + 1 - mx).start()
-    await_bytes(s.every.at[0], s.share_recv.at[2])
-
-    grads = s.every[...]
-    square = jnp.sum((grads * grads).reshape(N * CH // 8, 8, T), axis=0)
-    s.square[mine] = square
-    for j in range(1, quarter):
-        spot = s.square.at[mine]
-        remote(
-            spot, spot, s.share_send.at[3], s.share_recv.at[3], ch=lax.rem(mine + j, quarter)
-        ).start()
-    await_bytes(s.square.at[pl.ds(0, quarter - 1)], s.share_recv.at[3])
-    total = jnp.sum(s.square[...], axis=(0, 1), keepdims=True)[0]
-    total = jnp.sum(total, axis=1, keepdims=True)
+            if not last or i == 2:
+                push_out(i, g)
+
+        s.every[g, mx * 4 + my, mz] = compute_group(g, load, send, s)
+        share_column(g)
+    share_layer(0)
+    push_out(1, g)
+    push_out(0, g)
+    share_layer(g)
+    column = s.every[:, mx * 4 + my].reshape(2 * 8 * G, T)
+    at = mine * 8 + mx * 4 + my
+    s.square[at] = jnp.sum(column * column, axis=0, keepdims=True)
+
+    def push_square(j, _):
+        spot = s.square.at[at]
+        where = layer(lax.rem(at + j, layer_size))
+        remote(spot, spot, s.square_send, s.square_recv, **where).start()
+        return 0
+
+    lax.fori_loop(1, layer_size, push_square, 0)
+
+    await_bytes(s.square.at[pl.ds(0, layer_size - 1)], s.square_recv)
+    total = jnp.sum(jnp.sum(s.square[...], axis=0), axis=1, keepdims=True)
     scale = lax.rsqrt(total / float(2 * F * CH * N * quarter) + 1e-06)
+    for g in range(GROUPS):
+        await_bytes(s.every.at[g, pl.ds(0, 7)], s.share_recv.at[1, g])
     for y in range(4):
         for z in range(8):
             for x in range(2):
-                p = y * 16 + z * 2 + x
-                grad_ref[pl.ds(p * CH, CH), :] = s.every[x, y, z] * scale
+                for g in range(GROUPS):
+                    rows = pl.ds((y * 16 + z * 2 + x) * CH + g * G, G)
+                    s.sorted[rows, :] = s.every[g, x * 4 + y, z] * scale
+    for j in range(N * CH // T):
+        grad_ref[:, pl.ds(j * T, T)] = s.sorted[pl.ds(j * T, T), :].T
 
     for i in range(3):
         await_bytes(outputs[i], s.out_recv.at[i])
@@ -373,10 +394,17 @@
             await_bytes(s.came.at[i, g, pl.ds(0, N - 1)], s.in_send.at[i, g])
         for i in range(3):
             await_bytes(s.goes.at[i, g, pl.ds(0, N - 1)], s.out_send.at[i, g])
-    await_bytes(s.every.at[0, 0, pl.ds(0, 7)], s.share_send.at[0])
-    await_bytes(s.every.at[0, pl.ds(0, 3)], s.share_send.at[1])
-    await_bytes(s.every.at[0], s.share_send.at[2])
-    await_bytes(s.square.at[pl.ds(0, quarter - 1)], s.share_send.at[3])
+        await_bytes(s.every.at[g, 0, pl.ds(0, 7)], s.share_send.at[0, g])
+        await_bytes(s.every.at[g, pl.ds(0, 7)], s.share_send.at[1, g])
+    await_bytes(s.square.at[pl.ds(0, layer_size - 1)], s.square_send)
+
+
+def hand_over(*refs):
+    copies = [pltpu.make_async_copy(refs[i], refs[4 + i], refs[8].at[i]) for i in range(4)]
+    for copy in copies:
+        copy.start()
+    for copy in copies:
+        copy.wait()
 
 
 def body(quarter, value_in, gate_inner, gate_outer, out_grad, filter_proj, decay, frequency):
@@ -384,36 +412,56 @@
     scratch |= dict(
         came=pltpu.VMEM((4, GROUPS, N, G, T), bf16),
         goes=pltpu.VMEM((3, GROUPS, N, G, T), bf16),
-        every=pltpu.VMEM((2, 4, 8, CH, T), f32),
-        square=pltpu.VMEM((quarter, 8, T), f32),
+        every=pltpu.VMEM((GROUPS, 8, 8, G, T), f32),
+        sorted=pltpu.VMEM((N * CH, T), f32),
+        square=pltpu.VMEM((8 * quarter, 1, T), f32),
+        proj=pltpu.VMEM((2, F, filter_proj.shape[1]), bf16),
+        decay=pltpu.VMEM(decay.shape, f32),
+        freq=pltpu.VMEM((1, F), f32),
+        table_sem=pltpu.SemaphoreType.DMA((3,)),
         in_send=pltpu.SemaphoreType.DMA((4, GROUPS)),
         in_recv=pltpu.SemaphoreType.DMA((4, GROUPS)),
         out_send=pltpu.SemaphoreType.DMA((3, GROUPS)),
         out_recv=pltpu.SemaphoreType.DMA((3,)),
-        share_send=pltpu.SemaphoreType.DMA((4,)),
-        share_recv=pltpu.SemaphoreType.DMA((4,)),
+        share_send=pltpu.SemaphoreType.DMA((2, GROUPS)),
+        share_recv=pltpu.SemaphoreType.DMA((2, GROUPS)),
+        square_send=pltpu.SemaphoreType.DMA,
+        square_recv=pltpu.SemaphoreType.DMA,
     )
     local = jax.ShapeDtypeStruct(value_in.shape, bf16)
     anywhere, vmem = pl.BlockSpec(memory_space=pl.ANY), pl.BlockSpec(memory_space=pltpu.VMEM)
-    grad_value, grad_inner, grad_outer, grads = pl.pallas_call(
+    hbm = pl.BlockSpec(memory_space=pltpu.HBM)
+    results = pl.pallas_call(
         functools.partial(kernel, tuple(scratch), quarter),
-        out_shape=(local, local, local, jax.ShapeDtypeStruct((N * CH, T), f32)),
-        in_specs=[anywhere] * 4 + [vmem] * 3,
+        out_shape=(local, local, local, jax.ShapeDtypeStruct((T, N * CH), f32)),
+        in_specs=[hbm] * 7,
         out_specs=[anywhere] * 3 + [vmem],
         scratch_shapes=list(scratch.values()),
         compiler_params=pltpu.CompilerParams(
             collective_id=0, has_side_effects=True, vmem_limit_bytes=40 << 20
         ),
     )(
-        value_in,
-        gate_inner,
-        gate_outer,
-        out_grad,
-        jnp.transpose(filter_proj, (0, 2, 1)),
-        decay,
-        frequency.reshape(1, F),
+        *(
+            pltpu.with_memory_space_constraint(x, pltpu.HBM)
+            for x in (
+                value_in,
+                gate_inner,
+                gate_outer,
+                out_grad,
+                jnp.transpose(filter_proj, (0, 2, 1)),
+                decay,
+                frequency.reshape(1, F),
+            )
+        )
     )
-    filter_grad = jnp.transpose(grads.reshape(N * CH, 2, F), (1, 0, 2))
+    grad_value, grad_inner, grad_outer, grads = pl.pallas_call(
+        hand_over,
+        out_shape=tuple(jax.ShapeDtypeStruct(x.shape, x.dtype) for x in results),
+        in_specs=[vmem] * 4,
+        out_specs=[hbm] * 4,
+        scratch_shapes=[pltpu.SemaphoreType.DMA((4,))],
+    )(*(pltpu.with_memory_space_constraint(x, pltpu.VMEM) for x in results))
+    filter_grad = jnp.transpose(grads.reshape(2, F, N * CH), (0, 2, 1))
     return grad_value, grad_inner, grad_outer, filter_grad
 
 

time: 79.6 us -> 60.9 us (0.77)
  Pallas kernels: 69.5 us -> 60.2 us
  local copies, waits for them, and re-layouts: 9.19 us -> 0 us
    pallas_call x1, Pallas kernels: 69.5 us -> 59.1 us  [body(): pl.pallas_call(functools.partial(kernel, tuple(scratch), quarter), out_sh...]
    unnamed x17 -> x0, local copies, waits for them, and re-layouts: 8.2 us -> none
    pallas_call x0 -> x1, Pallas kernels: none -> 1.09 us  [body(): pl.pallas_call(hand_over, out_shape=tuple((jax.ShapeDtypeStruct(x.shape,...]
    pallas_call x1 -> x0, local copies, waits for them, and re-layouts: 1 us -> none  [body(): pl.pallas_call(functools.partial(kernel, tuple(scratch), quarter), out_sh...]
where the time goes in v1:
time: 60.9 us; the launch traced here: 60.8 us
  Pallas kernels  60.2 us (99%)
  between operations  0.64 us (1%)
    pallas_call x1, Pallas kernels, body(): pl.pallas_call(functools.partial(kernel, tuple(scratch), quarter), out_sh...  59.1 us

profile of v1, /device:TPU:1, one launch (start us, length us, event | category | flops | bytes accessed | tf_op | source)
XLA Modules:
  0.0 60.8 jit_solution(16272192579151173299)
XLA Ops:
  0.6 59.1 %shard_map.102 = (bf16[1024,128]{1,0:T(8,128)(2,1)S(1)}, bf16[1024,128]{1,0:T(8,128)(2,1)S(1)}, bf16[1024,128]{1,0:T(8,128)(2,1)S(1)}, f32[128,1024]{1,0:T(8,128)S(1)}) custom-call(bf16[1024,128]{1,0:T(8,128)(2,1)} %refs_0_.1, bf16[1024,128]{1,0:T(8,128)(2,1)} %refs_1_.1, bf16[1024,128]{1,0:T(8,128)(2,1)} %refs_2_.1, bf16[1024,128]{1,0:T(8,128)(2,1)} %refs_3_.1, ...), custom_call_target="tpu_custom_call" | custom-call | tf_op jit(solution)/shard_map/pallas_call | solution.py:434
  59.7 1.1 %shard_map.103 = (bf16[1024,128]{1,0:T(8,128)(2,1)}, bf16[1024,128]{1,0:T(8,128)(2,1)}, bf16[1024,128]{1,0:T(8,128)(2,1)}, f32[128,1024]{1,0:T(8,128)}) custom-call(bf16[1024,128]{1,0:T(8,128)(2,1)S(1)} %get-tuple-element.12.refs_0_, bf16[1024,128]{1,0:T(8,128)(2,1)S(1)} %get-tuple-element.13.refs_1_, bf16[1024,128]{1,0:T(8,128)(2,1)S(1)} %get-tuple-element.14.refs_2_, ...), custom_call_target="tpu_custom_call" | custom-call | tf_op jit(solution)/shard_map/pallas_call | solution.py:457

commit v2 on v1

--- a/solution.py
+++ b/solution.py
@@ -102,6 +102,38 @@
     lax.fori_loop(0, 2 * CH, toeplitz, 0, unroll=2)
 
 
+def encode(x):
+    top = jnp.maximum(jnp.max(jnp.abs(x), axis=-1, keepdims=True), 1e-35)
+    u = x / top
+    q = u * u
+    q = (q * q) * 2.0**60
+    q = q * q
+    return jnp.where(u < 0.0, -q, q).astype(bf16), top
+
+
+def decode(y, top):
+    y = y.astype(f32)
+    root = jnp.sqrt(jnp.sqrt(jnp.sqrt(jnp.abs(y)) * 2.0**-60))
+    root = jnp.where(y < 0.0, -root, jnp.where(y > 0.0, root, 0.0))
+    return root * top
+
+
+def to_lanes(top, first):
+    n, m, _ = top.shape
+    spot = lax.broadcasted_iota(jnp.int32, (n, m, T), 2) == first + lax.broadcasted_iota(
+        jnp.int32, (n, m, T), 1
+    )
+    return jnp.sum(jnp.where(spot, jnp.broadcast_to(top, (n, m, T)), 0.0), axis=1, keepdims=True)
+
+
+def from_lanes(row, first, m):
+    n = row.shape[0]
+    spot = lax.broadcasted_iota(jnp.int32, (n, m, T), 2) == first + lax.broadcasted_iota(
+        jnp.int32, (n, m, T), 1
+    )
+    return jnp.sum(jnp.where(spot, jnp.broadcast_to(row, (n, m, T)), 0.0), axis=2, keepdims=True)
+
+
 def of_channel(d):
     return pl.ds(d, N, stride=G)
 
@@ -203,9 +235,8 @@
     s.act[...] = inner_act
     s.mixed[...] = load(1) * inner_act
     outer_act = conv(1, g, s.mixed, False, s)
-    out_grad = load(3)
-    send(2, out_grad * outer_act)
-    s.x[...] = out_grad * load(2)
+    send(2, outer_act)
+    s.x[...] = load(2)
     grad_mixed, grad_outer = corr(1, g, s.x, s.mixed, False, s)
     send(1, grad_mixed * s.act[...])
     s.x[...] = grad_mixed * load(1)
@@ -255,12 +286,21 @@
 def kernel(names, quarter, *refs):
     inputs, refs = refs[:4], refs[4:]
     small = refs[:3]
-    outputs, grad_ref, refs = refs[3:6], refs[6], refs[7:]
+    outer_ref, inner_ref, grad_ref, refs = refs[3], refs[4], refs[5], refs[6:]
     s = SimpleNamespace(**dict(zip(names, refs)))
     me, mine = lax.axis_index("seq"), lax.axis_index("ch")
     mx, mz, my = lax.rem(me, 2), lax.rem(me // 2, 8), me // 16
 
     tables = (s.proj, s.decay, s.freq)
+
+    def packing(i, g):
+        if i >= 2:
+            return pltpu.make_async_copy(inputs[i], (s.gate, s.cotangent)[i - 2], s.pack_sem.at[0, i])
+        source = inputs[i].at[:, pl.ds(g * G, G), :]
+        return pltpu.make_async_copy(source, s.leaves.at[g, :, i], s.pack_sem.at[g, i])
+
+    for i, g in ((0, 0), (1, 0), (2, 0), (3, 0), (0, 1), (1, 1)):
+        packing(i, g).start()
     for i in range(3):
         pltpu.make_async_copy(small[i], tables[i], s.table_sem.at[i]).start()
     barrier = pltpu.get_barrier_semaphore()
@@ -284,48 +324,43 @@
     lax.fori_loop(8, layer_size, greet_layer, 0, unroll=8)
     pl.semaphore_wait(barrier, N - 1 + layer_size - 8)
 
-    def block_rows(p, g):
-        return pl.ds(pl.multiple_of(p * CH + g * G, G), G)
-
-    for g in range(GROUPS):
-        if g == 1:
-            for i in range(3):
-                pltpu.make_async_copy(small[i], tables[i], s.table_sem.at[i]).wait()
-            prepare(me * CH, *tables, s)
-        for i in (0, 1, 3, 2):
-
-            def push(j, _, g=g, i=i):
-                p = lax.rem(me + j, N)
-                remote(
-                    inputs[i].at[block_rows(p, g), :],
-                    s.came.at[i, g, me],
-                    s.in_send.at[i, g],
-                    s.in_recv.at[i, g],
-                    seq=p,
-                ).start()
-                return 0
-
-            lax.fori_loop(1, N, push, 0, unroll=9)
-            pltpu.make_async_copy(
-                inputs[i].at[block_rows(me, g), :], s.came.at[i, g, me], s.in_recv.at[i, g]
-            ).start()
-
-    def push_out(i, g):
+    def push_all(source, target, send, recv):
         def push(j, _):
             p = lax.rem(me + j, N)
-            remote(
-                s.goes.at[i, g, p],
-                outputs[i].at[block_rows(me, g), :],
-                s.out_send.at[i, g],
-                s.out_recv.at[i],
-                seq=p,
-            ).start()
+            remote(source.at[p], target.at[me], send, recv, seq=p).start()
             return 0
 
         lax.fori_loop(1, N, push, 0, unroll=9)
-        pltpu.make_async_copy(
-            s.goes.at[i, g, me], outputs[i].at[block_rows(me, g), :], s.out_recv.at[i]
-        ).start()
+        pltpu.make_async_copy(source.at[me], target.at[me], recv).start()
+
+    def push_in(g, k):
+        sems = s.in_send.at[g, k], s.in_recv.at[g, k]
+        if k == 0:
+            push_all(s.leaves.at[g], s.came.at[g], *sems)
+        else:
+            push_all(s.leaves_outer.at[g], s.came_outer.at[g], *sems)
+
+    def push_out(source, target, g, k):
+        push_all(source.at[g], target.at[g], s.out_send.at[g, k], s.out_recv.at[g, k])
+
+    packing(0, 0).wait()
+    packing(1, 0).wait()
+    push_in(0, 0)
+    packing(2, 0).wait()
+    packing(3, 0).wait()
+    product, top = encode(s.gate[...].astype(f32) * s.cotangent[...].astype(f32))
+    s.leaves_outer[0] = product[:, :G]
+    s.leaves_outer[1] = product[:, G:]
+    s.leaves_top[...] = to_lanes(top, 0)
+    push_all(s.leaves_top, s.came_top, s.top_send.at[0], s.top_recv.at[0])
+    push_in(0, 1)
+    for i in range(3):
+        pltpu.make_async_copy(small[i], tables[i], s.table_sem.at[i]).wait()
+    prepare(me * CH, *tables, s)
+    packing(0, 1).wait()
+    packing(1, 1).wait()
+    push_in(1, 0)
+    push_in(1, 1)
 
     def share_column(g):
         spot = s.every.at[g, mx * 4 + my, mz]
@@ -345,21 +380,34 @@
         here = set()
 
         def load(i, g=g, here=here):
-            if i not in here:
-                here.add(i)
-                await_bytes(s.came.at[i, g], s.in_recv.at[i, g])
-            return s.came[i, g].reshape(ROWS, T).astype(f32)
+            if i == 2:
+                if g == 0:
+                    await_bytes(s.came_top, s.top_recv.at[0])
+                await_bytes(s.came_outer.at[g], s.in_recv.at[g, 1])
+                top = from_lanes(s.came_top[...], g * G, G)
+                return decode(s.came_outer[g], top).reshape(ROWS, T)
+            if not here:
+                here.add(0)
+                await_bytes(s.came.at[g], s.in_recv.at[g, 0])
+            return s.came[g, :, i].reshape(ROWS, T).astype(f32)
 
         def send(i, val, g=g, last=last):
-            s.goes[i, g] = val.astype(bf16).reshape(N, G, T)
-            if not last or i == 2:
-                push_out(i, g)
+            if i == 2:
+                s.goes_outer[g], top = encode(val.reshape(N, G, T))
+                row = to_lanes(top, g * G)
+                s.goes_top[...] = row + s.goes_top[...] if g else row
+                push_out(s.goes_outer, s.back_outer, g, 0)
+                if last:
+                    push_all(s.goes_top, s.back_top, s.top_send.at[1], s.top_recv.at[1])
+                return
+            s.goes_inner[g, :, i] = val.astype(bf16).reshape(N, G, T)
+            if i == 0 and not last:
+                push_out(s.goes_inner, inner_ref, g, 1)
 
         s.every[g, mx * 4 + my, mz] = compute_group(g, load, send, s)
         share_column(g)
     share_layer(0)
-    push_out(1, g)
-    push_out(0, g)
+    push_out(s.goes_inner, inner_ref, g, 1)
     share_layer(g)
     column = s.every[:, mx * 4 + my].reshape(2 * 8 * G, T)
     at = mine * 8 + mx * 4 + my
@@ -372,6 +420,13 @@
         return 0
 
     lax.fori_loop(1, layer_size, push_square, 0)
+
+    await_bytes(s.back_top, s.top_recv.at[1])
+    for g in range(GROUPS):
+        await_bytes(s.back_outer.at[g], s.out_recv.at[g, 0])
+        rows = pl.ds(g * G, G)
+        outer_act = decode(s.back_outer[g], from_lanes(s.back_top[...], g * G, G))
+        outer_ref[:, rows, :] = (s.cotangent[:, rows, :].astype(f32) * outer_act).astype(bf16)
 
     await_bytes(s.square.at[pl.ds(0, layer_size - 1)], s.square_recv)
     total = jnp.sum(jnp.sum(s.square[...], axis=0), axis=1, keepdims=True)
@@ -387,20 +442,32 @@
     for j in range(N * CH // T):
         grad_ref[:, pl.ds(j * T, T)] = s.sorted[pl.ds(j * T, T), :].T
 
-    for i in range(3):
-        await_bytes(outputs[i], s.out_recv.at[i])
+    sent = pl.ds(0, N - 1)
+    for way in (0, 1):
+        await_bytes(s.back_top.at[sent], s.top_send.at[way])
     for g in range(GROUPS):
-        for i in range(4):
-            await_bytes(s.came.at[i, g, pl.ds(0, N - 1)], s.in_send.at[i, g])
-        for i in range(3):
-            await_bytes(s.goes.at[i, g, pl.ds(0, N - 1)], s.out_send.at[i, g])
+        await_bytes(inner_ref.at[g], s.out_recv.at[g, 1])
+        await_bytes(s.came.at[g, sent], s.in_send.at[g, 0])
+        await_bytes(s.came_outer.at[g, sent], s.in_send.at[g, 1])
+        await_bytes(s.goes_outer.at[g, sent], s.out_send.at[g, 0])
+        await_bytes(s.goes_inner.at[g, sent], s.out_send.at[g, 1])
         await_bytes(s.every.at[g, 0, pl.ds(0, 7)], s.share_send.at[0, g])
         await_bytes(s.every.at[g, pl.ds(0, 7)], s.share_send.at[1, g])
     await_bytes(s.square.at[pl.ds(0, layer_size - 1)], s.square_send)
 
 
-def hand_over(*refs):
-    copies = [pltpu.make_async_copy(refs[i], refs[4 + i], refs[8].at[i]) for i in range(4)]
+def hand_over(outer_ref, inner_ref, grad_ref, value_out, inner_out, outer_out, grad_out, sems):
+    copies = [pltpu.make_async_copy(grad_ref, grad_out, sems.at[6])]
+    for g in range(GROUPS):
+        rows = (slice(None), pl.ds(g * G, G), slice(None))
+        for i, (source, target) in enumerate(
+            (
+                (inner_ref.at[g, :, 0], value_out),
+                (inner_ref.at[g, :, 1], inner_out),
+                (outer_ref.at[rows], outer_out),
+            )
+        ):
+            copies.append(pltpu.make_async_copy(source, target.at[rows], sems.at[g * 3 + i]))
     for copy in copies:
         copy.start()
     for copy in copies:
@@ -410,8 +477,21 @@
 def body(quarter, value_in, gate_inner, gate_outer, out_grad, filter_proj, decay, frequency):
     scratch = {name: pltpu.VMEM(*spec) for name, spec in COMPUTE_SCRATCH.items()}
     scratch |= dict(
-        came=pltpu.VMEM((4, GROUPS, N, G, T), bf16),
-        goes=pltpu.VMEM((3, GROUPS, N, G, T), bf16),
+        gate=pltpu.VMEM((N, CH, T), bf16),
+        cotangent=pltpu.VMEM((N, CH, T), bf16),
+        leaves=pltpu.VMEM((GROUPS, N, 2, G, T), bf16),
+        came=pltpu.VMEM((GROUPS, N, 2, G, T), bf16),
+        leaves_outer=pltpu.VMEM((GROUPS, N, G, T), bf16),
+        came_outer=pltpu.VMEM((GROUPS, N, G, T), bf16),
+        back_outer=pltpu.VMEM((GROUPS, N, G, T), bf16),
+        leaves_top=pltpu.VMEM((N, 1, T), f32),
+        came_top=pltpu.VMEM((N, 1, T), f32),
+        goes_top=pltpu.VMEM((N, 1, T), f32),
+        back_top=pltpu.VMEM((N, 1, T), f32),
+        top_send=pltpu.SemaphoreType.DMA((2,)),
+        top_recv=pltpu.SemaphoreType.DMA((2,)),
+        goes_outer=pltpu.VMEM((GROUPS, N, G, T), bf16),
+        goes_inner=pltpu.VMEM((GROUPS, N, 2, G, T), bf16),
         every=pltpu.VMEM((GROUPS, 8, 8, G, T), f32),
         sorted=pltpu.VMEM((N * CH, T), f32),
         square=pltpu.VMEM((8 * quarter, 1, T), f32),
@@ -419,23 +499,29 @@
         decay=pltpu.VMEM(decay.shape, f32),
         freq=pltpu.VMEM((1, F), f32),
         table_sem=pltpu.SemaphoreType.DMA((3,)),
-        in_send=pltpu.SemaphoreType.DMA((4, GROUPS)),
-        in_recv=pltpu.SemaphoreType.DMA((4, GROUPS)),
-        out_send=pltpu.SemaphoreType.DMA((3, GROUPS)),
-        out_recv=pltpu.SemaphoreType.DMA((3,)),
+        pack_sem=pltpu.SemaphoreType.DMA((GROUPS, 4)),
+        in_send=pltpu.SemaphoreType.DMA((GROUPS, 2)),
+        in_recv=pltpu.SemaphoreType.DMA((GROUPS, 2)),
+        out_send=pltpu.SemaphoreType.DMA((GROUPS, 2)),
+        out_recv=pltpu.SemaphoreType.DMA((GROUPS, 2)),
         share_send=pltpu.SemaphoreType.DMA((2, GROUPS)),
         share_recv=pltpu.SemaphoreType.DMA((2, GROUPS)),
         square_send=pltpu.SemaphoreType.DMA,
         square_recv=pltpu.SemaphoreType.DMA,
     )
-    local = jax.ShapeDtypeStruct(value_in.shape, bf16)
+    local = jax.ShapeDtypeStruct((N, CH, T), bf16)
+    grad = jax.ShapeDtypeStruct((T, N * CH), f32)
     anywhere, vmem = pl.BlockSpec(memory_space=pl.ANY), pl.BlockSpec(memory_space=pltpu.VMEM)
     hbm = pl.BlockSpec(memory_space=pltpu.HBM)
     results = pl.pallas_call(
         functools.partial(kernel, tuple(scratch), quarter),
-        out_shape=(local, local, local, jax.ShapeDtypeStruct((T, N * CH), f32)),
+        out_shape=(
+            local,
+            jax.ShapeDtypeStruct((GROUPS, N, 2, G, T), bf16),
+            grad,
+        ),
         in_specs=[hbm] * 7,
-        out_specs=[anywhere] * 3 + [vmem],
+        out_specs=[vmem, anywhere, vmem],
         scratch_shapes=list(scratch.values()),
         compiler_params=pltpu.CompilerParams(
             collective_id=0, has_side_effects=True, vmem_limit_bytes=40 << 20
@@ -444,10 +530,7 @@
         *(
             pltpu.with_memory_space_constraint(x, pltpu.HBM)
             for x in (
-                value_in,
-                gate_inner,
-                gate_outer,
-                out_grad,
+                *(x.reshape(N, CH, T) for x in (value_in, gate_inner, gate_outer, out_grad)),
                 jnp.transpose(filter_proj, (0, 2, 1)),
                 decay,
                 frequency.reshape(1, F),
@@ -456,13 +539,14 @@
     )
     grad_value, grad_inner, grad_outer, grads = pl.pallas_call(
         hand_over,
-        out_shape=tuple(jax.ShapeDtypeStruct(x.shape, x.dtype) for x in results),
-        in_specs=[vmem] * 4,
+        out_shape=(local, local, local, grad),
+        in_specs=[vmem] * 3,
         out_specs=[hbm] * 4,
-        scratch_shapes=[pltpu.SemaphoreType.DMA((4,))],
+        scratch_shapes=[pltpu.SemaphoreType.DMA((7,))],
     )(*(pltpu.with_memory_space_constraint(x, pltpu.VMEM) for x in results))
     filter_grad = jnp.transpose(grads.reshape(2, F, N * CH), (0, 2, 1))
-    return grad_value, grad_inner, grad_outer, filter_grad
+    flat = tuple(x.reshape(N * CH, T) for x in (grad_value, grad_inner, grad_outer))
+    return (*flat, filter_grad)
 
 
 def solution(mesh):

time: 60.9 us -> 57.6 us (0.946)
  Pallas kernels: 60.2 us -> 56.8 us
    pallas_call x1, Pallas kernels: 59.1 us -> 55.7 us  [body(): pl.pallas_call(functools.partial(kernel, tuple(scratch), quarter), out_sh...]
where the time goes in v2:
time: 57.6 us; the launch traced here: 57.5 us
  Pallas kernels  56.8 us (99%)
  between operations  0.64 us (1%)
    pallas_call x1, Pallas kernels, body(): pl.pallas_call(functools.partial(kernel, tuple(scratch), quarter), out_sh...  55.7 us

profile of v2, /device:TPU:1, one launch (start us, length us, event | category | flops | bytes accessed | tf_op | source)
XLA Modules:
  0.0 57.5 jit_solution(7170178843517644402)
XLA Ops:
  0.6 55.7 %shard_map.102 = (bf16[64,16,128]{2,1,0:T(8,128)(2,1)S(1)}, bf16[2,64,2,8,128]{4,3,2,1,0:T(8,128)(2,1)S(1)}, f32[128,1024]{1,0:T(8,128)S(1)}) custom-call(bf16[64,16,128]{2,1,0:T(8,128)(2,1)} %bitcast.12, bf16[64,16,128]{2,1,0:T(8,128)(2,1)} %bitcast.13, bf16[64,16,128]{2,1,0:T(8,128)(2,1)} %bitcast.14, bf16[64,16,128]{2,1,0:T(8,128)(2,1)} %bitcast.15, ...), custom_call_target="tpu_custom_call" | custom-call | tf_op jit(solution)/shard_map/pallas_call | solution.py:516
  56.4 1.1 %shard_map.103 = (bf16[64,16,128]{2,1,0:T(8,128)(2,1)}, bf16[64,16,128]{2,1,0:T(8,128)(2,1)}, bf16[64,16,128]{2,1,0:T(8,128)(2,1)}, f32[128,1024]{1,0:T(8,128)}) custom-call(bf16[64,16,128]{2,1,0:T(8,128)(2,1)S(1)} %get-tuple-element.11.outer_ref, bf16[2,64,2,8,128]{4,3,2,1,0:T(8,128)(2,1)S(1)} %get-tuple-element.12.inner_ref, ...), custom_call_target="tpu_custom_call" | custom-call | tf_op jit(solution)/shard_map/pallas_call | solution.py:540

commit v3 on v2

--- a/solution.py
+++ b/solution.py
@@ -99,7 +99,7 @@
         s.toep_lo[i] = lo
         return 0
 
-    lax.fori_loop(0, 2 * CH, toeplitz, 0, unroll=2)
+    lax.fori_loop(0, 2 * CH, toeplitz, 0, unroll=4)
 
 
 def encode(x):
@@ -167,10 +167,10 @@
         return (re * zr - im * zi) + src[rows, :T], (re * zi + im * zr) + src[rows, T:]
 
     zero = jnp.zeros((G, T), f32)
-    end = lax.fori_loop(0, HALF, functools.partial(step, False), (zero, zero), unroll=8)
+    end = lax.fori_loop(0, HALF, functools.partial(step, False), (zero, zero), unroll=HALF)
     late = lanes((G, T)) < F if backward else lanes((G, T)) >= F
     begin = tuple(jnp.where(late, pltpu.roll(x, F, 1), 0.0) for x in end)
-    lax.fori_loop(0, HALF, functools.partial(step, True), begin, unroll=8)
+    lax.fori_loop(0, HALF, functools.partial(step, True), begin, unroll=HALF)
 
 
 def carried(state, weight, decay, which, s):
@@ -193,7 +193,7 @@
         s.y[of_channel(d), :] = y
         return 0
 
-    lax.fori_loop(0, G, channel, 0, unroll=4)
+    lax.fori_loop(0, G, channel, 0, unroll=8)
     return s.y[...] + carried(s.state[k], s.weight[k, grow, :], s.far[k, grow, :], 1, s)
 
 
@@ -219,7 +219,7 @@
         s.lag[pl.ds(d, 1), :] = jnp.sum(pairs, axis=0, keepdims=True)
         return 0
 
-    lax.fori_loop(0, G, channel, 0, unroll=4)
+    lax.fori_loop(0, G, channel, 0, unroll=8)
     both = s.local[:, :T] * s.state[k, :, T:] + s.local[:, T:] * s.state[k, :, :T]
     both = jnp.sum(both.reshape(HALF, G, T), axis=0)
     both = both + pltpu.roll(both, F, 1)
@@ -299,10 +299,8 @@
         source = inputs[i].at[:, pl.ds(g * G, G), :]
         return pltpu.make_async_copy(source, s.leaves.at[g, :, i], s.pack_sem.at[g, i])
 
-    for i, g in ((0, 0), (1, 0), (2, 0), (3, 0), (0, 1), (1, 1)):
-        packing(i, g).start()
-    for i in range(3):
-        pltpu.make_async_copy(small[i], tables[i], s.table_sem.at[i]).start()
+    packing(0, 0).start()
+    packing(1, 0).start()
     barrier = pltpu.get_barrier_semaphore()
 
     def greet(j, _):
@@ -322,6 +320,10 @@
     layer_size = 8 * quarter
     lax.fori_loop(1, N, greet, 0, unroll=9)
     lax.fori_loop(8, layer_size, greet_layer, 0, unroll=8)
+    for i, g in ((2, 0), (3, 0), (0, 1), (1, 1)):
+        packing(i, g).start()
+    for i in range(3):
+        pltpu.make_async_copy(small[i], tables[i], s.table_sem.at[i]).start()
     pl.semaphore_wait(barrier, N - 1 + layer_size - 8)
 
     def push_all(source, target, send, recv):
@@ -404,12 +406,12 @@
             if i == 0 and not last:
                 push_out(s.goes_inner, inner_ref, g, 1)
 
-        s.every[g, mx * 4 + my, mz] = compute_group(g, load, send, s)
+        s.every[g, mx * 4 + my, mz] = compute_group(g, load, send, s).astype(bf16)
         share_column(g)
     share_layer(0)
     push_out(s.goes_inner, inner_ref, g, 1)
     share_layer(g)
-    column = s.every[:, mx * 4 + my].reshape(2 * 8 * G, T)
+    column = s.every[:, mx * 4 + my].astype(f32).reshape(2 * 8 * G, T)
     at = mine * 8 + mx * 4 + my
     s.square[at] = jnp.sum(column * column, axis=0, keepdims=True)
 
@@ -438,7 +440,7 @@
             for x in range(2):
                 for g in range(GROUPS):
                     rows = pl.ds((y * 16 + z * 2 + x) * CH + g * G, G)
-                    s.sorted[rows, :] = s.every[g, x * 4 + y, z] * scale
+                    s.sorted[rows, :] = s.every[g, x * 4 + y, z].astype(f32) * scale
     for j in range(N * CH // T):
         grad_ref[:, pl.ds(j * T, T)] = s.sorted[pl.ds(j * T, T), :].T
 
@@ -492,7 +494,7 @@
         top_recv=pltpu.SemaphoreType.DMA((2,)),
         goes_outer=pltpu.VMEM((GROUPS, N, G, T), bf16),
         goes_inner=pltpu.VMEM((GROUPS, N, 2, G, T), bf16),
-        every=pltpu.VMEM((GROUPS, 8, 8, G, T), f32),
+        every=pltpu.VMEM((GROUPS, 8, 8, G, T), bf16),
         sorted=pltpu.VMEM((N * CH, T), f32),
         square=pltpu.VMEM((8 * quarter, 1, T), f32),
         proj=pltpu.VMEM((2, F, filter_proj.shape[1]), bf16),

time: 57.6 us -> 54.7 us (0.950)
  Pallas kernels: 56.8 us -> 54 us
    pallas_call x1, Pallas kernels: 55.7 us -> 52.9 us  [body(): pl.pallas_call(functools.partial(kernel, tuple(scratch), quarter), out_sh...]
where the time goes in v3:
time: 54.7 us; the launch traced here: 54.6 us
  Pallas kernels  54 us (99%)
  between operations  0.64 us (1%)
    pallas_call x1, Pallas kernels, body(): pl.pallas_call(functools.partial(kernel, tuple(scratch), quarter), out_sh...  52.9 us
    pallas_call x1, Pallas kernels, body(): pl.pallas_call(hand_over, out_shape=(local, local, local, grad), in_specs...  1.1 us

profile of v3, /device:TPU:1, one launch (start us, length us, event | category | flops | bytes accessed | tf_op | source)
XLA Modules:
  0.0 54.6 jit_solution(1883621972902437703)
XLA Ops:
  0.6 52.9 %shard_map.102 = (bf16[64,16,128]{2,1,0:T(8,128)(2,1)S(1)}, bf16[2,64,2,8,128]{4,3,2,1,0:T(8,128)(2,1)S(1)}, f32[128,1024]{1,0:T(8,128)S(1)}) custom-call(bf16[64,16,128]{2,1,0:T(8,128)(2,1)} %bitcast.12, bf16[64,16,128]{2,1,0:T(8,128)(2,1)} %bitcast.13, bf16[64,16,128]{2,1,0:T(8,128)(2,1)} %bitcast.14, bf16[64,16,128]{2,1,0:T(8,128)(2,1)} %bitcast.15, ...), custom_call_target="tpu_custom_call" | custom-call | tf_op jit(solution)/shard_map/pallas_call | solution.py:518
  53.5 1.1 %shard_map.103 = (bf16[64,16,128]{2,1,0:T(8,128)(2,1)}, bf16[64,16,128]{2,1,0:T(8,128)(2,1)}, bf16[64,16,128]{2,1,0:T(8,128)(2,1)}, f32[128,1024]{1,0:T(8,128)}) custom-call(bf16[64,16,128]{2,1,0:T(8,128)(2,1)S(1)} %get-tuple-element.11.outer_ref, bf16[2,64,2,8,128]{4,3,2,1,0:T(8,128)(2,1)S(1)} %get-tuple-element.12.inner_ref, ...), custom_call_target="tpu_custom_call" | custom-call | tf_op jit(solution)/shard_map/pallas_call | solution.py:542

commit v4 on v3

--- a/solution.py
+++ b/solution.py
@@ -408,8 +408,8 @@
 
         s.every[g, mx * 4 + my, mz] = compute_group(g, load, send, s).astype(bf16)
         share_column(g)
+    push_out(s.goes_inner, inner_ref, g, 1)
     share_layer(0)
-    push_out(s.goes_inner, inner_ref, g, 1)
     share_layer(g)
     column = s.every[:, mx * 4 + my].astype(f32).reshape(2 * 8 * G, T)
     at = mine * 8 + mx * 4 + my

time: 54.7 us -> 54.5 us (level)
  no operation moved by 1% of the time
where the time goes in v4:
time: 54.5 us; the launch traced here: 54.4 us
  Pallas kernels  53.7 us (99%)
  between operations  0.64 us (1%)
    pallas_call x1, Pallas kernels, body(): pl.pallas_call(functools.partial(kernel, tuple(scratch), quarter), out_sh...  52.6 us
    pallas_call x1, Pallas kernels, body(): pl.pallas_call(hand_over, out_shape=(local, local, local, grad), in_specs...  1.1 us

profile of v4, /device:TPU:1, one launch (start us, length us, event | category | flops | bytes accessed | tf_op | source)
XLA Modules:
  0.0 54.4 jit_solution(5608816510941449324)
XLA Ops:
  0.6 52.6 %shard_map.102 = (bf16[64,16,128]{2,1,0:T(8,128)(2,1)S(1)}, bf16[2,64,2,8,128]{4,3,2,1,0:T(8,128)(2,1)S(1)}, f32[128,1024]{1,0:T(8,128)S(1)}) custom-call(bf16[64,16,128]{2,1,0:T(8,128)(2,1)} %bitcast.12, bf16[64,16,128]{2,1,0:T(8,128)(2,1)} %bitcast.13, bf16[64,16,128]{2,1,0:T(8,128)(2,1)} %bitcast.14, bf16[64,16,128]{2,1,0:T(8,128)(2,1)} %bitcast.15, ...), custom_call_target="tpu_custom_call" | custom-call | tf_op jit(solution)/shard_map/pallas_call | solution.py:518
  53.3 1.1 %shard_map.103 = (bf16[64,16,128]{2,1,0:T(8,128)(2,1)}, bf16[64,16,128]{2,1,0:T(8,128)(2,1)}, bf16[64,16,128]{2,1,0:T(8,128)(2,1)}, f32[128,1024]{1,0:T(8,128)}) custom-call(bf16[64,16,128]{2,1,0:T(8,128)(2,1)S(1)} %get-tuple-element.11.outer_ref, bf16[2,64,2,8,128]{4,3,2,1,0:T(8,128)(2,1)S(1)} %get-tuple-element.12.inner_ref, ...), custom_call_target="tpu_custom_call" | custom-call | tf_op jit(solution)/shard_map/pallas_call | solution.py:542
